TPU v7x, 512 devices: a whole 4x4x16 slice. The times are simulated.
512 devices in a mesh: tiles: 128 (over y, z, core), samp: 4 (over x).
Axes of the slice: x: 4, y: 4, z: 16, core: 2. Of those that a mesh axis runs over, the one named last changes fastest.
Arguments:
- samples: bfloat16 [256, 131072], P('samp', 'tiles'), may hold values from -6 to 6
- omega: float32 [1280, 512, 512], P('tiles', 'samp'), may hold values from -1 to 2, as said below
- coords: int32 [1280, 2], P('tiles'), may hold values from 0 to 255, as said below
Outputs:
- updated: float32 [1280, 512, 512], P('tiles', 'samp')
Inputs may be any that keep to these rules, and one draw needn't show every extreme that they name: `coords`: tile k lies with index k // 10 of tiles. Write d for that index, and blocks d * 2 to (d + 1) * 2 - 1 as its own blocks; indices of devices wrap around. The first 2 tiles of d are the diagonal tiles (I, I) of its own blocks in order. Each other tile of d is (I, J) with I an own block and J a block of d + 1, or I a block of d - 1 and J a block of d + 1, or I < J both own blocks. No unordered pair of blocks appears twice in the whole list. `omega`: tiles with I == J are symmetric with diagonal entries from 0.5 to 2.
All inputs are finite; a program needn't handle non-finite values.
Results may differ from a plain program's by a relative error of at most 0.0023.
Values may be sent and summed in bfloat16 or wider, within the bound.
No kernel may reach another device: no remote copies, remote signals or barrier semaphores. Data moves between devices by JAX's collectives and lax.ppermute only.
A program may use at most 64 MiB of HBM per device.

v0:
```python
import jax
import jax.numpy as jnp
from jax import lax
from jax.sharding import PartitionSpec as P

BLK_DEV = 2
ITERS = 2
step_size = 0.25
penalty = 0.2


def with_halo(shard, sides, width):
    for axis, dim in sides:
        size, length = (lax.axis_size(axis), shard.shape[dim])
        up = [(i, (i + 1) % size) for i in range(size)]
        down = [(j, i) for i, j in up]
        last = lax.slice_in_dim(shard, length - width, length, axis=dim)
        leading = lax.slice_in_dim(shard, 0, width, axis=dim)
        before = lax.ppermute(last, axis, up)
        after = lax.ppermute(leading, axis, down)
        shard = jnp.concatenate([before, shard, after], axis=dim)
    return shard


def columns(matrix, start, count):
    return lax.dynamic_slice_in_dim(matrix, start, count, 1)


def add_columns(totals, block, start):
    current = lax.dynamic_slice_in_dim(totals, start, block.shape[1], 1)
    return lax.dynamic_update_slice_in_dim(totals, current + block, start, 1)


def shards(samples, omega, coords):
    quarter = lax.axis_index("samp")
    tile_rows = omega.shape[1]
    width = omega.shape[2]
    own_width = samples.shape[1]
    blocks_all = BLK_DEV * lax.axis_size("tiles")
    first_block = (lax.axis_index("tiles") - 1) * BLK_DEV
    local = (coords - first_block + blocks_all) % blocks_all
    off_diagonal = (coords[:, 0] != coords[:, 1]).astype(jnp.float32)
    offset = quarter * tile_rows
    full_rows = lax.all_gather(samples, "samp", axis=0, tiled=True)
    sample_win = with_halo(full_rows, (("tiles", 1),), own_width)
    count = sample_win.shape[0]
    row_ids = offset + lax.broadcasted_iota(jnp.int32, (tile_rows, width), 0)
    col_ids = lax.broadcasted_iota(jnp.int32, (tile_rows, width), 1)
    diagonal_cells = row_ids == col_ids
    contract_cols = (((1,), (1,)), ((), ()))
    contract_rows = (((0,), (0,)), ((), ()))
    for iteration in range(ITERS):
        omega_low = omega.astype(jnp.bfloat16)
        totals = jnp.zeros((count, 3 * own_width), jnp.float32)
        for tile_slot in range(omega.shape[0]):
            row_start = local[tile_slot, 0] * width
            col_start = local[tile_slot, 1] * width
            rows_low = omega_low[tile_slot]
            row_part = columns(sample_win, row_start + offset, tile_rows)
            col_block = columns(sample_win, col_start, width)
            to_col = jnp.dot(row_part, rows_low, preferred_element_type=jnp.float32)
            to_row = lax.dot_general(
                col_block, rows_low, contract_cols, preferred_element_type=jnp.float32
            )
            totals = add_columns(totals, to_col, col_start)
            totals = add_columns(totals, to_row * off_diagonal[tile_slot], row_start + offset)
        returned = with_halo(totals, (("tiles", 1),), own_width)
        partial_value = (
            totals[:, own_width : 2 * own_width]
            + returned[:, :own_width]
            + returned[:, 4 * own_width :]
        )
        summed = lax.psum(partial_value, "samp")
        product_own = summed.astype(jnp.bfloat16)
        product_win = with_halo(product_own, (("tiles", 1),), own_width)
        new_tiles = []
        for tile_slot in range(omega.shape[0]):
            row_start = local[tile_slot, 0] * width
            col_start = local[tile_slot, 1] * width
            product_rows = columns(product_win, row_start + offset, tile_rows)
            sample_rows = columns(sample_win, row_start + offset, tile_rows)
            sample_cols = columns(sample_win, col_start, width)
            product_cols = columns(product_win, col_start, width)
            first = lax.dot_general(
                product_rows, sample_cols, contract_rows, preferred_element_type=jnp.float32
            )
            second = lax.dot_general(
                sample_rows, product_cols, contract_rows, preferred_element_type=jnp.float32
            )
            grad = (first + second) / (2.0 * count)
            value = omega[tile_slot] - step_size * grad
            shrunk = jnp.sign(value) * jnp.maximum(jnp.abs(value) - step_size * penalty, 0.0)
            positive = 0.5 * (value + jnp.sqrt(value * value + 4.0 * step_size))
            same_block = coords[tile_slot, 0] == coords[tile_slot, 1]
            new_tiles.append(jnp.where(diagonal_cells & same_block, positive, shrunk))
        omega = jnp.stack(new_tiles)
    return omega


def solution(mesh):
    in_specs = (P("samp", "tiles"), P("tiles", "samp", None), P("tiles", None))
    out_specs = P("tiles", "samp", None)
    return jax.shard_map(shards, mesh=mesh, in_specs=in_specs, out_specs=out_specs, check_vma=False)
```

profile of v0, /device:TPU:4, one launch (start us, length us, event | category | flops | bytes accessed | tf_op | source)
XLA Modules:
  0.0 228.5 jit_solution(8097895202772696019)
XLA Ops:
  0.0 16.8 %all_gather.3 = bf16[256,1024]{1,0:T(8,128)(2,1)S(1)} all-gather(bf16[64,1024]{1,0:T(8,128)(2,1)} %param.3), channel_id=1, replica_groups=mesh['tiles'=128,'samp'=4] {'samp'}, dimensions={0}, use_global_device_ids=true | all-gather | bytes 655360 | tf_op jit(solution)/shard_map/all_gather | solution.py:44
  16.8 1.9 collective-permute-start
  18.7 7.0 %collective-permute-start.1 = (bf16[256,1024]{1,0:T(8,128)(2,1)S(1)}, bf16[256,1024]{1,0:T(8,128)(2,1)}, u32[]{:S(2)}, u32[]{:S(2)}) collective-permute-start(bf16[256,1024]{1,0:T(8,128)(2,1)S(1)} %all_gather.3), channel_id=1, source_target_pairs={{4,0},{8,4},{12,8},{16,12},{20,16},{24,20},{28,24},{32,28},{36,32}... | collective-permute-start | bytes 1572872 | tf_op jit(solution)/shard_map/ppermute | solution.py:20
  40.3 1.9 convert_element_type.14
  43.1 1.1 constant_dynamic-update-slice_fusion.2
  44.2 1.1 constant_dynamic-update-slice_fusion
  45.9 0.9 add_dynamic-update-slice_fusion.19
  49.1 0.9 add_dynamic-update-slice_fusion.17
  51.2 0.9 add_dynamic-update-slice_fusion.15
  55.5 0.9 add_dynamic-update-slice_fusion.11
  56.7 1.9 collective-permute-start.2
  58.6 7.0 %collective-permute-start.3 = (f32[256,1024]{1,0:T(8,128)S(1)}, f32[256,1024]{1,0:T(8,128)S(1)}, u32[]{:S(2)}, u32[]{:S(2)}) collective-permute-start(f32[256,1024]{1,0:T(8,128)S(1)} %get-tuple-element.8), channel_id=1, source_target_pairs={{4,0},{8,4},{12,8},{16,12},{20,16},{24,20},{28,24},{32,28},{36,32}... | collective-permute-start | bytes 3145736 | tf_op jit(solution)/shard_map/ppermute | solution.py:20
  65.6 10.5 %collective-permute-done.2 = f32[256,1024]{1,0:T(8,128)S(1)} collective-permute-done((f32[256,1024]{1,0:T(8,128)S(1)}, f32[256,1024]{1,0:T(8,128)S(1)}, u32[]{:S(2)}, u32[]{:S(2)}) %collective-permute-start.2) | collective-permute-done | bytes 1048608 | tf_op jit(solution)/shard_map/ppermute | solution.py:19
  76.1 1.8 collective-permute-done.3
  78.2 28.7 %all-reduce.2 = bf16[256,1024]{1,0:T(8,128)(2,1)S(1)} all-reduce(f32[256,1024]{1,0:T(8,128)S(1)} %fusion.61), channel_id=1, replica_groups=mesh['tiles'=128,'samp'=4] {'samp'}, use_global_device_ids=true, to_apply=%region_0.1 | all-reduce | flops 262144 | bytes 1572864 | tf_op jit(solution)/shard_map/psum | solution.py:73
  106.9 1.9 collective-permute-start.4
  108.8 7.1 %collective-permute-start.5 = (bf16[256,1024]{1,0:T(8,128)(2,1)S(1)}, bf16[256,1024]{1,0:T(8,128)(2,1)S(1)}, u32[]{:S(2)}, u32[]{:S(2)}) collective-permute-start(bf16[256,1024]{1,0:T(8,128)(2,1)S(1)} %all-reduce.2), channel_id=1, source_target_pairs={{4,0},{8,4},{12,8},{16,12},{20,16},{24,20},{28,24},{32,28},{36,32}... | collective-permute-start | bytes 1572872 | tf_op jit(solution)/shard_map/ppermute | solution.py:20
  133.9 0.9 add_dynamic-update-slice_fusion.10
  138.7 0.9 add_dynamic-update-slice_fusion.8
  141.9 0.9 add_dynamic-update-slice_fusion.6
  148.8 0.9 add_dynamic-update-slice_fusion.2
  149.9 1.9 collective-permute-start.6
  151.9 7.0 %collective-permute-start.7 = (f32[256,1024]{1,0:T(8,128)S(1)}, f32[256,1024]{1,0:T(8,128)S(1)}, u32[]{:S(2)}, u32[]{:S(2)}) collective-permute-start(f32[256,1024]{1,0:T(8,128)S(1)} %get-tuple-element.6), channel_id=1, source_target_pairs={{4,0},{8,4},{12,8},{16,12},{20,16},{24,20},{28,24},{32,28},{36,32}... | collective-permute-start | bytes 3145736 | tf_op jit(solution)/shard_map/ppermute | solution.py:20
  158.8 10.5 %collective-permute-done.6 = f32[256,1024]{1,0:T(8,128)S(1)} collective-permute-done((f32[256,1024]{1,0:T(8,128)S(1)}, f32[256,1024]{1,0:T(8,128)S(1)}, u32[]{:S(2)}, u32[]{:S(2)}) %collective-permute-start.6) | collective-permute-done | bytes 1048608 | tf_op jit(solution)/shard_map/ppermute | solution.py:19
  169.4 1.8 collective-permute-done.7
  171.4 31.7 %all-reduce.3 = bf16[256,1024]{1,0:T(8,128)(2,1)S(1)} all-reduce(f32[256,1024]{1,0:T(8,128)S(1)} %fusion.60), channel_id=1, replica_groups=mesh['tiles'=128,'samp'=4] {'samp'}, use_global_device_ids=true, to_apply=%region_1.2 | all-reduce | flops 262144 | bytes 1572864 | tf_op jit(solution)/shard_map/psum | solution.py:73
  203.1 1.9 collective-permute-start.8
  205.1 7.2 %collective-permute-start.9 = (bf16[256,1024]{1,0:T(8,128)(2,1)S(1)}, bf16[256,1024]{1,0:T(8,128)(2,1)S(1)}, u32[]{:S(2)}, u32[]{:S(2)}) collective-permute-start(bf16[256,1024]{1,0:T(8,128)(2,1)S(1)} %all-reduce.3), channel_id=1, source_target_pairs={{4,0},{8,4},{12,8},{16,12},{20,16},{24,20},{28,24},{32,28},{36,32}... | collective-permute-start | bytes 1572872 | tf_op jit(solution)/shard_map/ppermute | solution.py:20
  212.2 4.7 %collective-permute-done.8 = bf16[256,1024]{1,0:T(8,128)(2,1)S(1)} collective-permute-done((bf16[256,1024]{1,0:T(8,128)(2,1)S(1)}, bf16[256,1024]{1,0:T(8,128)(2,1)S(1)}, u32[]{:S(2)}, u32[]{:S(2)}) %collective-permute-start.8) | collective-permute-done | bytes 524320 | tf_op jit(solution)/shard_map/ppermute | solution.py:19
  216.9 1.8 collective-permute-done.9
  225.8 1.5 copy-done.20
  227.3 1.2 bitcast_dynamic-update-slice_fusion
  (133 shorter events, 35.2 us)
Async XLA Ops:
  16.8 26.3 %collective-permute-start = (bf16[256,1024]{1,0:T(8,128)(2,1)S(1)}, bf16[256,1024]{1,0:T(8,128)(2,1)}, u32[]{:S(2)}, u32[]{:S(2)}) collective-permute-start(bf16[256,1024]{1,0:T(8,128)(2,1)S(1)} %all_gather.3), channel_id=1, source_target_pairs={{0,4},{4,8},{8,12},{12,16},{16,20},{20,24},{24,28},{28,32},{32,36}... | collective-permute-start | bytes 1572872 | tf_op jit(solution)/shard_map/ppermute | solution.py:19
  18.7 25.5 %collective-permute-start.1 = (bf16[256,1024]{1,0:T(8,128)(2,1)S(1)}, bf16[256,1024]{1,0:T(8,128)(2,1)}, u32[]{:S(2)}, u32[]{:S(2)}) collective-permute-start(bf16[256,1024]{1,0:T(8,128)(2,1)S(1)} %all_gather.3), channel_id=1, source_target_pairs={{4,0},{8,4},{12,8},{16,12},{20,16},{24,20},{28,24},{32,28},{36,32}... | collective-permute-start | bytes 1572872 | tf_op jit(solution)/shard_map/ppermute | solution.py:20
  40.3 2.1 copy-start.19
  56.7 19.4 %collective-permute-start.2 = (f32[256,1024]{1,0:T(8,128)S(1)}, f32[256,1024]{1,0:T(8,128)S(1)}, u32[]{:S(2)}, u32[]{:S(2)}) collective-permute-start(f32[256,1024]{1,0:T(8,128)S(1)} %get-tuple-element.7), channel_id=1, source_target_pairs={{0,4},{4,8},{8,12},{12,16},{16,20},{20,24},{24,28},{28,32},{32,36}... | collective-permute-start | bytes 3145736 | tf_op jit(solution)/shard_map/ppermute | solution.py:19
  58.6 19.3 %collective-permute-start.3 = (f32[256,1024]{1,0:T(8,128)S(1)}, f32[256,1024]{1,0:T(8,128)S(1)}, u32[]{:S(2)}, u32[]{:S(2)}) collective-permute-start(f32[256,1024]{1,0:T(8,128)S(1)} %get-tuple-element.8), channel_id=1, source_target_pairs={{4,0},{8,4},{12,8},{16,12},{20,16},{24,20},{28,24},{32,28},{36,32}... | collective-permute-start | bytes 3145736 | tf_op jit(solution)/shard_map/ppermute | solution.py:20
  106.9 22.9 %collective-permute-start.4 = (bf16[256,1024]{1,0:T(8,128)(2,1)S(1)}, bf16[256,1024]{1,0:T(8,128)(2,1)S(1)}, u32[]{:S(2)}, u32[]{:S(2)}) collective-permute-start(bf16[256,1024]{1,0:T(8,128)(2,1)S(1)} %all-reduce.2), channel_id=1, source_target_pairs={{0,4},{4,8},{8,12},{12,16},{16,20},{20,24},{24,28},{28,32},{32,36}... | collective-permute-start | bytes 1572872 | tf_op jit(solution)/shard_map/ppermute | solution.py:19
  108.8 21.0 %collective-permute-start.5 = (bf16[256,1024]{1,0:T(8,128)(2,1)S(1)}, bf16[256,1024]{1,0:T(8,128)(2,1)S(1)}, u32[]{:S(2)}, u32[]{:S(2)}) collective-permute-start(bf16[256,1024]{1,0:T(8,128)(2,1)S(1)} %all-reduce.2), channel_id=1, source_target_pairs={{4,0},{8,4},{12,8},{16,12},{20,16},{24,20},{28,24},{32,28},{36,32}... | collective-permute-start | bytes 1572872 | tf_op jit(solution)/shard_map/ppermute | solution.py:20
  131.1 1.7 copy-start
  135.2 1.6 copy-start.3
  136.9 1.5 copy-start.5
  138.4 1.7 copy-start.7
  140.1 1.5 copy-start.9
  141.6 1.7 copy-start.11
  143.3 1.6 copy-start.13
  144.9 1.5 copy-start.15
  146.5 1.6 copy-start.17
  148.1 0.7 copy-start.1
  149.9 19.4 %collective-permute-start.6 = (f32[256,1024]{1,0:T(8,128)S(1)}, f32[256,1024]{1,0:T(8,128)S(1)}, u32[]{:S(2)}, u32[]{:S(2)}) collective-permute-start(f32[256,1024]{1,0:T(8,128)S(1)} %get-tuple-element.5), channel_id=1, source_target_pairs={{0,4},{4,8},{8,12},{12,16},{16,20},{20,24},{24,28},{28,32},{32,36}... | collective-permute-start | bytes 3145736 | tf_op jit(solution)/shard_map/ppermute | solution.py:19
  151.9 19.3 %collective-permute-start.7 = (f32[256,1024]{1,0:T(8,128)S(1)}, f32[256,1024]{1,0:T(8,128)S(1)}, u32[]{:S(2)}, u32[]{:S(2)}) collective-permute-start(f32[256,1024]{1,0:T(8,128)S(1)} %get-tuple-element.6), channel_id=1, source_target_pairs={{4,0},{8,4},{12,8},{16,12},{20,16},{24,20},{28,24},{32,28},{36,32}... | collective-permute-start | bytes 3145736 | tf_op jit(solution)/shard_map/ppermute | solution.py:20
  203.1 13.8 %collective-permute-start.8 = (bf16[256,1024]{1,0:T(8,128)(2,1)S(1)}, bf16[256,1024]{1,0:T(8,128)(2,1)S(1)}, u32[]{:S(2)}, u32[]{:S(2)}) collective-permute-start(bf16[256,1024]{1,0:T(8,128)(2,1)S(1)} %all-reduce.3), channel_id=1, source_target_pairs={{0,4},{4,8},{8,12},{12,16},{16,20},{20,24},{24,28},{28,32},{32,36}... | collective-permute-start | bytes 1572872 | tf_op jit(solution)/shard_map/ppermute | solution.py:19
  205.1 13.6 %collective-permute-start.9 = (bf16[256,1024]{1,0:T(8,128)(2,1)S(1)}, bf16[256,1024]{1,0:T(8,128)(2,1)S(1)}, u32[]{:S(2)}, u32[]{:S(2)}) collective-permute-start(bf16[256,1024]{1,0:T(8,128)(2,1)S(1)} %all-reduce.3), channel_id=1, source_target_pairs={{4,0},{8,4},{12,8},{16,12},{20,16},{24,20},{28,24},{32,28},{36,32}... | collective-permute-start | bytes 1572872 | tf_op jit(solution)/shard_map/ppermute | solution.py:20
  220.4 1.2 copy-start.4
  220.9 1.3 copy-start.6
  221.6 1.0 copy-start.8
  222.1 1.0 copy-start.10
  222.7 1.0 copy-start.12
  223.2 1.0 copy-start.14
  223.7 1.0 copy-start.16
  224.2 1.0 copy-start.18
  224.8 2.5 %copy-start.2 = (f32[128,512]{1,0:T(8,128)S(1)}, f32[128,512]{1,0:T(8,128)}, u32[]{:S(2)}) copy-start(f32[128,512]{1,0:T(8,128)} %copy-done.1) | copy-start | bytes 786436
  225.8 1.5 copy-start.20
where the time goes:
time: 230 us; the launch traced here: 228 us
  blocking collectives  77.2 us (34%)
  starting transfers between devices  44.8 us (19%)
  matrix products  36.4 us (16%)
  waiting for transfers between devices  31.1 us (14%)
  between operations  26.3 us (11%)
  local copies, waits for them, and re-layouts  9.34 us (4%)
  other arithmetic  3.42 us (1%)
    psum x2, blocking collectives, shards(): summed = lax.psum(partial_value, 'samp')  60.4 us
    ppermute x5, starting transfers between devices, with_halo(): after = lax.ppermute(leading, axis, down)  35.2 us
    ppermute x5, waiting for transfers between devices, with_halo(): before = lax.ppermute(last, axis, up)  25.8 us
    dot_general x20, matrix products, shards(): lax.dot_general(col_block, rows_low, contract_cols, preferred_element_typ...  17 us
    all_gather x1, blocking collectives, shards(): full_rows = lax.all_gather(samples, 'samp', axis=0, tiled=True)  16.8 us
    dot_general x20, matrix products, shards(): lax.dot_general(product_rows, sample_cols, contract_rows, preferred_eleme...  10.6 us
    ppermute x5, starting transfers between devices, with_halo(): before = lax.ppermute(last, axis, up)  9.59 us
    ppermute x5, waiting for transfers between devices, with_halo(): after = lax.ppermute(leading, axis, down)  5.27 us
  transfers between devices with their start and end apart: 10, of which 6 were waited for; matrix products, arithmetic and copies ran while one was open for 3% of the time, Pallas kernels for 0%

commit v1 on v0

--- a/solution.py
+++ b/solution.py
@@ -70,7 +70,9 @@
             + returned[:, :own_width]
             + returned[:, 4 * own_width :]
         )
-        summed = lax.psum(partial_value, "samp")
+        summed = partial_value
+        for hop in (1, 2):
+            summed = summed + lax.ppermute(summed, "samp", [(dev, dev ^ hop) for dev in range(4)])
         product_own = summed.astype(jnp.bfloat16)
         product_win = with_halo(product_own, (("tiles", 1),), own_width)
         new_tiles = []

time: 230 us -> 266 us (1.16)
  the two profiles are of different devices: /device:TPU:4 before, /device:TPU:30 now
where the time goes in v1:
time: 266 us; the launch traced here: 265 us
  waiting for transfers between devices  112 us (42%)
  starting transfers between devices  65.4 us (25%)
  matrix products  37.7 us (14%)
  between operations  25.9 us (10%)
  blocking collectives  13.6 us (5%)
  local copies, waits for them, and re-layouts  6.13 us (2%)
  other arithmetic  3.95 us (1%)
    ppermute x4, waiting for transfers between devices, shards(): lax.ppermute(summed, 'samp', [(dev, dev ^ hop) for dev in range(4)])  81.2 us
    ppermute x5, starting transfers between devices, with_halo(): after = lax.ppermute(leading, axis, down)  47.6 us
    ppermute x5, waiting for transfers between devices, with_halo(): before = lax.ppermute(last, axis, up)  25.8 us
    dot_general x20, matrix products, shards(): lax.dot_general(col_block, rows_low, contract_cols, preferred_element_typ...  17.4 us
    all_gather x1, blocking collectives, shards(): full_rows = lax.all_gather(samples, 'samp', axis=0, tiled=True)  13.6 us
    dot_general x20, matrix products, shards(): lax.dot_general(product_rows, sample_cols, contract_rows, preferred_eleme...  10 us
    ppermute x5, starting transfers between devices, with_halo(): before = lax.ppermute(last, axis, up)  9.59 us
    ppermute x4, starting transfers between devices, shards(): lax.ppermute(summed, 'samp', [(dev, dev ^ hop) for dev in range(4)])  8.24 us
  transfers between devices with their start and end apart: 14, of which 10 were waited for; matrix products, arithmetic and copies ran while one was open for 2% of the time, Pallas kernels for 0%

profile of v1, /device:TPU:30, one launch (start us, length us, event | category | flops | bytes accessed | tf_op | source)
XLA Modules:
  0.0 265.0 jit_solution(7979956825956479500)
XLA Ops:
  0.0 13.6 %all_gather.3 = bf16[256,1024]{1,0:T(8,128)(2,1)S(1)} all-gather(bf16[64,1024]{1,0:T(8,128)(2,1)} %param.3), channel_id=1, replica_groups=mesh['tiles'=128,'samp'=4] {'samp'}, dimensions={0}, use_global_device_ids=true | all-gather | bytes 655360 | tf_op jit(solution)/shard_map/all_gather | solution.py:44
  13.6 1.9 collective-permute-start
  15.5 7.6 %collective-permute-start.1 = (bf16[256,1024]{1,0:T(8,128)(2,1)S(1)}, bf16[256,1024]{1,0:T(8,128)(2,1)S(1)}, u32[]{:S(2)}, u32[]{:S(2)}) collective-permute-start(bf16[256,1024]{1,0:T(8,128)(2,1)S(1)} %all_gather.3), channel_id=1, source_target_pairs={{4,0},{8,4},{12,8},{16,12},{20,16},{24,20},{28,24},{32,28},{36,32}... | collective-permute-start | bytes 1572872 | tf_op jit(solution)/shard_map/ppermute | solution.py:20
  37.7 1.9 convert_element_type.14
  42.2 0.9 fusion.59
  45.7 0.9 add_dynamic-update-slice_fusion.16
  52.6 1.9 collective-permute-start.2
  54.5 6.1 %collective-permute-start.3 = (f32[256,1024]{0,1:T(8,128)S(1)}, f32[256,1024]{0,1:T(8,128)S(1)}, u32[]{:S(2)}, u32[]{:S(2)}) collective-permute-start(f32[256,1024]{0,1:T(8,128)S(1)} %get-tuple-element.8), channel_id=1, source_target_pairs={{4,0},{8,4},{12,8},{16,12},{20,16},{24,20},{28,24},{32,28},{36,32}... | collective-permute-start | bytes 3145736 | tf_op jit(solution)/shard_map/ppermute | solution.py:20
  60.6 10.5 %collective-permute-done.2 = f32[256,1024]{0,1:T(8,128)S(1)} collective-permute-done((f32[256,1024]{0,1:T(8,128)S(1)}, f32[256,1024]{0,1:T(8,128)S(1)}, u32[]{:S(2)}, u32[]{:S(2)}) %collective-permute-start.2) | collective-permute-done | bytes 1048608 | tf_op jit(solution)/shard_map/ppermute | solution.py:19
  71.1 1.8 collective-permute-done.3
  73.1 2.4 collective-permute-start.4
  75.5 22.4 %collective-permute-done.4 = f32[256,1024]{0,1:T(8,128)S(1)} collective-permute-done((f32[256,1024]{0,1:T(8,128)S(1)}, f32[256,1024]{0,1:T(8,128)S(1)}, u32[]{:S(2)}, u32[]{:S(2)}) %collective-permute-start.4) | collective-permute-done | bytes 1048608 | tf_op jit(solution)/shard_map/ppermute | solution.py:75
  98.0 1.9 collective-permute-start.5
  100.0 20.1 %collective-permute-done.5 = f32[256,1024]{0,1:T(8,128)S(1)} collective-permute-done((f32[256,1024]{0,1:T(8,128)S(1)}, f32[256,1024]{0,1:T(8,128)S(1)}, u32[]{:S(2)}, u32[]{:S(2)}) %collective-permute-start.5) | collective-permute-done | bytes 1048608 | tf_op jit(solution)/shard_map/ppermute | solution.py:75
  120.3 1.9 collective-permute-start.6
  122.3 13.8 %collective-permute-start.7 = (bf16[256,1024]{0,1:T(8,128)(2,1)S(1)}, bf16[256,1024]{0,1:T(8,128)(2,1)S(1)}, u32[]{:S(2)}, u32[]{:S(2)}) collective-permute-start(bf16[256,1024]{0,1:T(8,128)(2,1)S(1)} %add_convert_fusion.1), channel_id=1, source_target_pairs={{4,0},{8,4},{12,8},{16,12},{20,16},{24,20},{28,24},{32,28},{36,32}... | collective-permute-start | bytes 1572872 | tf_op jit(solution)/shard_map/ppermute | solution.py:20
  155.5 0.9 fusion.57
  160.4 0.9 add_dynamic-update-slice_fusion.7
  169.6 1.9 collective-permute-start.8
  171.5 5.8 %collective-permute-start.9 = (f32[256,1024]{0,1:T(8,128)S(1)}, f32[256,1024]{0,1:T(8,128)S(1)}, u32[]{:S(2)}, u32[]{:S(2)}) collective-permute-start(f32[256,1024]{0,1:T(8,128)S(1)} %get-tuple-element.6), channel_id=1, source_target_pairs={{4,0},{8,4},{12,8},{16,12},{20,16},{24,20},{28,24},{32,28},{36,32}... | collective-permute-start | bytes 3145736 | tf_op jit(solution)/shard_map/ppermute | solution.py:20
  177.3 10.5 %collective-permute-done.8 = f32[256,1024]{0,1:T(8,128)S(1)} collective-permute-done((f32[256,1024]{0,1:T(8,128)S(1)}, f32[256,1024]{0,1:T(8,128)S(1)}, u32[]{:S(2)}, u32[]{:S(2)}) %collective-permute-start.8) | collective-permute-done | bytes 1048608 | tf_op jit(solution)/shard_map/ppermute | solution.py:19
  187.8 1.8 collective-permute-done.9
  189.8 2.0 collective-permute-start.10
  191.8 22.4 %collective-permute-done.10 = f32[256,1024]{0,1:T(8,128)S(1)} collective-permute-done((f32[256,1024]{0,1:T(8,128)S(1)}, f32[256,1024]{0,1:T(8,128)S(1)}, u32[]{:S(2)}, u32[]{:S(2)}) %collective-permute-start.10) | collective-permute-done | bytes 1048608 | tf_op jit(solution)/shard_map/ppermute | solution.py:75
  214.3 1.9 collective-permute-start.11
  216.2 16.3 %collective-permute-done.11 = f32[256,1024]{0,1:T(8,128)S(1)} collective-permute-done((f32[256,1024]{0,1:T(8,128)S(1)}, f32[256,1024]{0,1:T(8,128)S(1)}, u32[]{:S(2)}, u32[]{:S(2)}) %collective-permute-start.11) | collective-permute-done | bytes 1048608 | tf_op jit(solution)/shard_map/ppermute | solution.py:75
  232.7 1.9 collective-permute-start.12
  234.6 14.4 %collective-permute-start.13 = (bf16[256,1024]{0,1:T(8,128)(2,1)S(1)}, bf16[256,1024]{0,1:T(8,128)(2,1)S(1)}, u32[]{:S(2)}, u32[]{:S(2)}) collective-permute-start(bf16[256,1024]{0,1:T(8,128)(2,1)S(1)} %add_convert_fusion), channel_id=1, source_target_pairs={{4,0},{8,4},{12,8},{16,12},{20,16},{24,20},{28,24},{32,28},{36,32}... | collective-permute-start | bytes 1572872 | tf_op jit(solution)/shard_map/ppermute | solution.py:20
  249.1 4.7 %collective-permute-done.12 = bf16[256,1024]{0,1:T(8,128)(2,1)S(1)} collective-permute-done((bf16[256,1024]{0,1:T(8,128)(2,1)S(1)}, bf16[256,1024]{0,1:T(8,128)(2,1)S(1)}, u32[]{:S(2)}, u32[]{:S(2)}) %collective-permute-start.12) | collective-permute-done | bytes 524320 | tf_op jit(solution)/shard_map/ppermute | solution.py:19
  253.8 1.8 collective-permute-done.13
  262.3 1.5 copy-done.2
  263.8 1.2 bitcast_dynamic-update-slice_fusion
  (107 shorter events, 39.6 us)
Async XLA Ops:
  13.6 26.9 %collective-permute-start = (bf16[256,1024]{1,0:T(8,128)(2,1)S(1)}, bf16[256,1024]{1,0:T(8,128)(2,1)S(1)}, u32[]{:S(2)}, u32[]{:S(2)}) collective-permute-start(bf16[256,1024]{1,0:T(8,128)(2,1)S(1)} %all_gather.3), channel_id=1, source_target_pairs={{0,4},{4,8},{8,12},{12,16},{16,20},{20,24},{24,28},{28,32},{32,36}... | collective-permute-start | bytes 1572872 | tf_op jit(solution)/shard_map/ppermute | solution.py:19
  15.5 25.1 %collective-permute-start.1 = (bf16[256,1024]{1,0:T(8,128)(2,1)S(1)}, bf16[256,1024]{1,0:T(8,128)(2,1)S(1)}, u32[]{:S(2)}, u32[]{:S(2)}) collective-permute-start(bf16[256,1024]{1,0:T(8,128)(2,1)S(1)} %all_gather.3), channel_id=1, source_target_pairs={{4,0},{8,4},{12,8},{16,12},{20,16},{24,20},{28,24},{32,28},{36,32}... | collective-permute-start | bytes 1572872 | tf_op jit(solution)/shard_map/ppermute | solution.py:20
  37.7 2.1 copy-start.1
  52.6 18.5 %collective-permute-start.2 = (f32[256,1024]{0,1:T(8,128)S(1)}, f32[256,1024]{0,1:T(8,128)S(1)}, u32[]{:S(2)}, u32[]{:S(2)}) collective-permute-start(f32[256,1024]{0,1:T(8,128)S(1)} %get-tuple-element.7), channel_id=1, source_target_pairs={{0,4},{4,8},{8,12},{12,16},{16,20},{20,24},{24,28},{28,32},{32,36}... | collective-permute-start | bytes 3145736 | tf_op jit(solution)/shard_map/ppermute | solution.py:19
  54.5 18.4 %collective-permute-start.3 = (f32[256,1024]{0,1:T(8,128)S(1)}, f32[256,1024]{0,1:T(8,128)S(1)}, u32[]{:S(2)}, u32[]{:S(2)}) collective-permute-start(f32[256,1024]{0,1:T(8,128)S(1)} %get-tuple-element.8), channel_id=1, source_target_pairs={{4,0},{8,4},{12,8},{16,12},{20,16},{24,20},{28,24},{32,28},{36,32}... | collective-permute-start | bytes 3145736 | tf_op jit(solution)/shard_map/ppermute | solution.py:20
  73.1 24.8 %collective-permute-start.4 = (f32[256,1024]{0,1:T(8,128)S(1)}, f32[256,1024]{0,1:T(8,128)S(1)}, u32[]{:S(2)}, u32[]{:S(2)}) collective-permute-start(f32[256,1024]{0,1:T(8,128)S(1)} %fusion.61), channel_id=1, source_target_pairs={{0,1},{1,0},{2,3},{3,2},{4,5},{5,4},{6,7},{7,6},{8,9},{9,8},{10,11... | collective-permute-start | bytes 3145736 | tf_op jit(solution)/shard_map/ppermute | solution.py:75
  98.0 22.1 %collective-permute-start.5 = (f32[256,1024]{0,1:T(8,128)S(1)}, f32[256,1024]{0,1:T(8,128)S(1)}, u32[]{:S(2)}, u32[]{:S(2)}) collective-permute-start(f32[256,1024]{0,1:T(8,128)S(1)} %add.361), channel_id=1, source_target_pairs={{0,2},{1,3},{2,0},{3,1},{4,6},{5,7},{6,4},{7,5},{8,10},{9,11},{10,... | collective-permute-start | bytes 3145736 | tf_op jit(solution)/shard_map/ppermute | solution.py:75
  120.3 29.5 %collective-permute-start.6 = (bf16[256,1024]{0,1:T(8,128)(2,1)S(1)}, bf16[256,1024]{0,1:T(8,128)(2,1)S(1)}, u32[]{:S(2)}, u32[]{:S(2)}) collective-permute-start(bf16[256,1024]{0,1:T(8,128)(2,1)S(1)} %add_convert_fusion.1), channel_id=1, source_target_pairs={{0,4},{4,8},{8,12},{12,16},{16,20},{20,24},{24,28},{28,32},{32,36}... | collective-permute-start | bytes 1572872 | tf_op jit(solution)/shard_map/ppermute | solution.py:19
  122.3 27.6 %collective-permute-start.7 = (bf16[256,1024]{0,1:T(8,128)(2,1)S(1)}, bf16[256,1024]{0,1:T(8,128)(2,1)S(1)}, u32[]{:S(2)}, u32[]{:S(2)}) collective-permute-start(bf16[256,1024]{0,1:T(8,128)(2,1)S(1)} %add_convert_fusion.1), channel_id=1, source_target_pairs={{4,0},{8,4},{12,8},{16,12},{20,16},{24,20},{28,24},{32,28},{36,32}... | collective-permute-start | bytes 1572872 | tf_op jit(solution)/shard_map/ppermute | solution.py:20
  151.1 1.7 copy-start
  169.6 18.2 %collective-permute-start.8 = (f32[256,1024]{0,1:T(8,128)S(1)}, f32[256,1024]{0,1:T(8,128)S(1)}, u32[]{:S(2)}, u32[]{:S(2)}) collective-permute-start(f32[256,1024]{0,1:T(8,128)S(1)} %get-tuple-element.5), channel_id=1, source_target_pairs={{0,4},{4,8},{8,12},{12,16},{16,20},{20,24},{24,28},{28,32},{32,36}... | collective-permute-start | bytes 3145736 | tf_op jit(solution)/shard_map/ppermute | solution.py:19
  171.5 18.1 %collective-permute-start.9 = (f32[256,1024]{0,1:T(8,128)S(1)}, f32[256,1024]{0,1:T(8,128)S(1)}, u32[]{:S(2)}, u32[]{:S(2)}) collective-permute-start(f32[256,1024]{0,1:T(8,128)S(1)} %get-tuple-element.6), channel_id=1, source_target_pairs={{4,0},{8,4},{12,8},{16,12},{20,16},{24,20},{28,24},{32,28},{36,32}... | collective-permute-start | bytes 3145736 | tf_op jit(solution)/shard_map/ppermute | solution.py:20
  189.8 24.3 %collective-permute-start.10 = (f32[256,1024]{0,1:T(8,128)S(1)}, f32[256,1024]{0,1:T(8,128)S(1)}, u32[]{:S(2)}, u32[]{:S(2)}) collective-permute-start(f32[256,1024]{0,1:T(8,128)S(1)} %fusion.60), channel_id=1, source_target_pairs={{0,1},{1,0},{2,3},{3,2},{4,5},{5,4},{6,7},{7,6},{8,9},{9,8},{10,11... | collective-permute-start | bytes 3145736 | tf_op jit(solution)/shard_map/ppermute | solution.py:75
  214.3 18.2 %collective-permute-start.11 = (f32[256,1024]{0,1:T(8,128)S(1)}, f32[256,1024]{0,1:T(8,128)S(1)}, u32[]{:S(2)}, u32[]{:S(2)}) collective-permute-start(f32[256,1024]{0,1:T(8,128)S(1)} %add.801), channel_id=1, source_target_pairs={{0,2},{1,3},{2,0},{3,1},{4,6},{5,7},{6,4},{7,5},{8,10},{9,11},{10,... | collective-permute-start | bytes 3145736 | tf_op jit(solution)/shard_map/ppermute | solution.py:75
  232.7 21.1 %collective-permute-start.12 = (bf16[256,1024]{0,1:T(8,128)(2,1)S(1)}, bf16[256,1024]{0,1:T(8,128)(2,1)S(1)}, u32[]{:S(2)}, u32[]{:S(2)}) collective-permute-start(bf16[256,1024]{0,1:T(8,128)(2,1)S(1)} %add_convert_fusion), channel_id=1, source_target_pairs={{0,4},{4,8},{8,12},{12,16},{16,20},{20,24},{24,28},{28,32},{32,36}... | collective-permute-start | bytes 1572872 | tf_op jit(solution)/shard_map/ppermute | solution.py:19
  234.6 20.9 %collective-permute-start.13 = (bf16[256,1024]{0,1:T(8,128)(2,1)S(1)}, bf16[256,1024]{0,1:T(8,128)(2,1)S(1)}, u32[]{:S(2)}, u32[]{:S(2)}) collective-permute-start(bf16[256,1024]{0,1:T(8,128)(2,1)S(1)} %add_convert_fusion), channel_id=1, source_target_pairs={{4,0},{8,4},{12,8},{16,12},{20,16},{24,20},{28,24},{32,28},{36,32}... | collective-permute-start | bytes 1572872 | tf_op jit(solution)/shard_map/ppermute | solution.py:20
  262.3 1.5 copy-start.2
